TPU v7x, 32 devices: a whole 2x2x4 slice. The times are simulated.
32 devices in a mesh: arc: 8 (over y, x, core), par: 4 (over z).
Axes of the slice: x: 2, y: 2, z: 4, core: 2. Of those that a mesh axis runs over, the one named last changes fastest.
Arguments:
- partials: bfloat16 [8, 3, 128, 8192], P('arc', None, 'par'), may hold values from -6 to 6
- epoch_index: int32 [8, 128], P('arc'), may hold values from 0 to 511, as said below
- whitening: float32 [8, 3, 128, 128], P('arc'), may hold values from -2 to 2, as said below
Outputs:
- normal_matrix: float32 [8192, 8192], P('arc', 'par')
Inputs may be any that keep to these rules, and one draw needn't show every extreme that they name: `epoch_index`: in each arc the epoch indices rise strictly; the first is 0 and the last is 511. `whitening`: each block is lower triangular with diagonal entries between 1 and 2.
All inputs are finite; a program needn't handle non-finite values.
Results may differ from a plain program's by a relative error of at most 0.0003.
Values may be sent and summed in bfloat16 or wider, within the bound.
No kernel may reach another device: no remote copies, remote signals or barrier semaphores. Data moves between devices by JAX's collectives and lax.ppermute only.
A program may use at most 128 MiB of HBM per device.

v0:
```python
import math
import jax
import jax.numpy as jnp
from jax import lax
from jax.sharding import PartitionSpec as P

KERNEL_GAIN = 8.0


def from_root(block, axis, owner):
    block = jnp.where(lax.axis_index(axis) == owner, block, jnp.zeros_like(block))
    return lax.psum(block, axis)


def mixing_matrices(epoch_index, whitening, epochs, row_scale):
    times_arc = epoch_index.astype(jnp.float32) / jnp.float32(4 * epochs - 1)
    later_time = times_arc[:, :, None]
    earlier_time = times_arc[:, None, :]
    green_part = jnp.minimum(later_time, earlier_time) * (
        1.0 - jnp.maximum(later_time, earlier_time)
    )
    kernel = jnp.eye(epochs, dtype=jnp.float32)[None] + KERNEL_GAIN / epochs * green_part
    mixing = jnp.einsum("acij,ajk->acik", whitening, kernel, precision=lax.Precision.HIGHEST)
    return mixing * row_scale


def on_device(partials, epoch_index, whitening):
    arc_local = partials.shape[0]
    epochs = epoch_index.shape[1]
    param_count = partials.shape[3]
    arc_count = lax.axis_size("arc")
    par_count = lax.axis_size("par")
    total_arcs = arc_local * arc_count
    col_block = param_count // par_count
    row_block = param_count // arc_count
    row_scale = 1.0 / math.sqrt(3 * epochs * total_arcs)
    mixing = mixing_matrices(epoch_index, whitening, epochs, row_scale)
    columns = lax.all_to_all(partials, "par", split_axis=3, concat_axis=2, tiled=True)
    arc_position = lax.axis_index("arc")
    holder = arc_position * row_block // col_block
    offset = arc_position * row_block - holder * col_block
    raw_cols = lax.all_gather(columns, "arc", axis=0, tiled=True)
    all_mixing = lax.all_gather(mixing, "arc", axis=0, tiled=True)
    gathered = jnp.einsum(
        "acij,acjk->acik", all_mixing, raw_cols.astype(jnp.float32), precision=lax.Precision.HIGHEST
    )
    raw_piece = lax.dynamic_slice_in_dim(raw_cols, offset, row_block, 3)
    raw_rows = from_root(raw_piece, "par", holder)
    row_data = jnp.einsum(
        "acij,acjk->acik", all_mixing, raw_rows.astype(jnp.float32), precision=lax.Precision.HIGHEST
    )
    row_flat = row_data.reshape(-1, row_block)
    col_flat = gathered.reshape(-1, col_block)
    return lax.dot_general(
        row_flat,
        col_flat,
        (((0,), (0,)), ((), ())),
        precision=lax.Precision.HIGHEST,
        preferred_element_type=jnp.float32,
    )


def solution(mesh):
    placed = (P("arc", None, "par", None), P("arc", None), P("arc", None, None, None))
    return jax.shard_map(
        on_device, mesh=mesh, in_specs=placed, out_specs=P("arc", "par"), check_vma=False
    )
```

profile of v0, /device:TPU:0, one launch (start us, length us, event | category | flops | bytes accessed | tf_op | source)
XLA Modules:
  0.0 509.8 jit_solution(11392306326867929905)
XLA Ops:
  6.5 0.0 all-gather.4.cloned.1.call-start
  6.5 10.6 %copy.9 = bf16[1,3,32,8192]{2,1,0,3:T(4,128)(2,1)} copy(bf16[1,3,32,8192]{3,2,1,0:T(8,128)(2,1)} %param.3) | data formatting | bytes 3145728 | tf_op args[0]
  17.2 7.4 %reshape.216 = bf16[4,2,98304]{2,1,0:T(2,128)(2,1)S(1)} reshape(bf16[8192,1,3,32]{3,2,1,0:T(4,128)(2,1)} %bitcast.29) | data formatting | bytes 3145728
  24.6 43.1 %all_to_all.18 = bf16[4,2,98304]{2,1,0:T(2,128)(2,1)S(1)} all-to-all(bf16[4,2,98304]{2,1,0:T(2,128)(2,1)S(1)} %reshape.216), channel_id=1, replica_groups=mesh['arc'=8,'par'=4] {'par'}, dimensions={0} | all-to-all | bytes 3145728 | tf_op jit(solution)/shard_map/all_to_all | solution.py:38
  67.7 7.0 %reshape.217 = bf16[8192,1,3,32]{3,2,1,0:T(4,128)(2,1)} reshape(bf16[4,2,98304]{2,1,0:T(2,128)(2,1)S(1)} %all_to_all.18) | data formatting | bytes 3145728
  74.8 11.6 %copy.15 = bf16[1,3,32,4,2048]{4,3,2,1,0:T(4,128)(2,1)S(1)} copy(bf16[1,3,32,4,2048]{2,1,4,3,0:T(4,128)(2,1)} %bitcast.28) | data formatting | bytes 3145728 | tf_op jit(solution)/shard_map/all_to_all | solution.py:38
  86.4 2.0 copy.11
  88.4 0.0 all-gather.4.cloned.1.call-update
  88.4 0.0 all-gather.6.cloned.1.call-start
  88.4 0.0 copy-done.3
  88.5 0.0 copy-done
  88.5 0.4 fusion
  88.9 0.8 copy.8
  89.7 0.0 all-gather.6.cloned.1.call-update
  89.7 0.2 all-reduce.2.cloned.1.call-start
  90.0 69.7 %all-gather.4.cloned.1.call-done = bf16[8,3,128,2048]{3,2,1,0:T(8,128)(2,1)} async-done(((bf16[1,3,128,2048]{3,2,1,0:T(8,128)(2,1)}), bf16[8,3,128,2048]{3,2,1,0:T(8,128)(2,1)}) %all-gather.4.cloned.1.call-update) | async-done | bytes 12582928 | tf_op jit(solution)/shard_map/all_gather | solution.py:42
  159.7 7.5 %dynamic-slice_select_fusion = bf16[8,3,128,1024]{3,2,1,0:T(8,128)(2,1)} fusion(bf16[8,3,128,2048]{3,2,1,0:T(8,128)(2,1)} %all-gather.4.cloned.1.call-done, s32[]{:T(128)S(6)} %select_n.18, pred[]{:T(512)S(6)} %eq.22), kind=kLoop, calls=%fused_computation | loop fusion | flops 3145728 | bytes 12582917 | tf_op jit(solution)/shard_map/jit(_where)/select_n | solution.py:11
  167.2 0.0 all-reduce.2.cloned.1.call-update
  167.2 19.9 %all-gather.6.cloned.1.call-done = f32[24,128,128]{2,1,0:T(8,128)} async-done(((f32[3,128,128]{2,1,0:T(8,128)}), f32[24,128,128]{2,1,0:T(8,128)}) %all-gather.6.cloned.1.call-update) | async-done | bytes 1572880 | tf_op jit(solution)/shard_map/all_gather | solution.py:43
  187.2 18.1 %fusion.17 = f32[8,3,128,2048]{3,2,1,0:T(8,128)} fusion(f32[8,3,128,128]{3,2,1,0:T(8,128)} %bitcast.30, bf16[8,3,128,2048]{3,2,1,0:T(8,128)(2,1)} %all-gather.4.cloned.1.call-done), kind=kOutput, calls=%fused_computation.22 | convolution fusion | flops 9663676416 | bytes 39321600 | tf_op jit(solution)/shard_map/acij,acjk->acik/dot_general | solution.py:44
  205.3 207.1 %all-reduce.2.cloned.1.call-done = bf16[8,3,128,1024]{3,2,1,0:T(8,128)(2,1)} async-done(((bf16[8,3,128,1024]{3,2,1,0:T(8,128)(2,1)}), bf16[8,3,128,1024]{3,2,1,0:T(8,128)(2,1)}) %all-reduce.2.cloned.1.call-update) | async-done | bytes 6291472 | tf_op jit(solution)/shard_map/psum | solution.py:12
  412.4 8.3 %fusion.16 = f32[8,3,128,1024]{2,3,1,0:T(8,128)S(1)} fusion(f32[8,3,128,128]{3,2,1,0:T(8,128)S(1)} %bitcast.31, bf16[8,3,128,1024]{3,2,1,0:T(8,128)(2,1)} %all-reduce.2.cloned.1.call-done), kind=kOutput, calls=%fused_computation.21 | convolution fusion | flops 4831838208 | bytes 20447232 | tf_op jit(solution)/shard_map/acij,acjk->acik/dot_general | solution.py:49
  420.8 0.0 copy-start.1
  420.8 82.4 %convolution_bitcast_fusion = f32[1024,2048]{1,0:T(8,128)} fusion(f32[8,3,128,1024]{2,3,1,0:T(8,128)S(1)} %fusion.16, f32[8,3,128,2048]{3,2,1,0:T(8,128)} %fusion.17), kind=kOutput, calls=%fused_computation.1 | convolution fusion | flops 77309411328 | bytes 46137344 | tf_op jit(solution)/shard_map/dot_general | solution.py:54
  (6 shorter events, 0.0 us)
Async XLA Ops:
  6.5 81.9 %copy-start = (f32[1,3,128,128]{3,2,1,0:T(8,128)S(1)}, f32[1,3,128,128]{3,2,1,0:T(8,128)}, u32[]{:S(2)}) copy-start(f32[1,3,128,128]{3,2,1,0:T(8,128)} %param.5) | copy-start | bytes 589828
  6.5 153.2 %all-gather.4.cloned.1.call-start = ((), (), s32[]{:S(2)}) async-start(), calls=%async_computation.1 | async-start | bytes 14155776 | tf_op jit(solution)/shard_map/all_gather | solution.py:42
  74.8 13.7 %copy-start.3 = (s32[1,128]{1,0:T(1,128)S(1)}, s32[1,128]{1,0:T(1,128)}, u32[]{:S(2)}) copy-start(s32[1,128]{1,0:T(1,128)} %param.4) | copy-start | bytes 1540
  88.4 98.8 %all-gather.6.cloned.1.call-start = ((), (), s32[]{:S(2)}) async-start(), calls=%async_computation.3 | async-start | bytes 1769472 | tf_op jit(solution)/shard_map/all_gather | solution.py:43
  89.7 322.7 %all-reduce.2.cloned.1.call-start = ((), (), s32[]{:S(2)}) async-start(), calls=%async_computation.2 | async-start | bytes 12582912 | tf_op jit(solution)/shard_map/psum | solution.py:12
  187.2 225.3 %copy-start.2 = (f32[24,128,128]{2,1,0:T(8,128)S(1)}, f32[24,128,128]{2,1,0:T(8,128)}, u32[]{:S(2)}) copy-start(f32[24,128,128]{2,1,0:T(8,128)} %all-gather.6.cloned.1.call-done) | copy-start | bytes 4718596
  420.8 82.4 %copy-start.1 = (f32[1,3,128,128]{3,2,1,0:T(8,128)S(1)}, f32[1,3,128,128]{3,2,1,0:T(8,128)}, u32[]{:S(2)}) copy-start(f32[1,3,128,128]{3,2,1,0:T(8,128)} %param.5) | copy-start | bytes 589828
Sparse Core Ops, SparseCore 0:
  88.5 71.1 all-gather.3
  161.6 25.5 all-gather.5
  189.5 222.8 all-reduce.1
where the time goes:
time: 511 us; the launch traced here: 510 us
  waiting for transfers between devices  297 us (58%)
  matrix products  109 us (21%)
  blocking collectives  43.1 us (8%)
  local copies, waits for them, and re-layouts  39.5 us (8%)
  between operations  13.2 us (3%)
  other arithmetic  7.54 us (1%)
    psum x1, waiting for transfers between devices, from_root(): return lax.psum(block, axis)  207 us
    dot_general x1, matrix products, on_device(): lax.dot_general(row_flat, col_flat, (((0,), (0,)), ((), ())), precision=l...  82.4 us
    all_gather x1, waiting for transfers between devices, on_device(): raw_cols = lax.all_gather(columns, 'arc', axis=0, tiled=True)  69.7 us
    all_to_all x1, blocking collectives, on_device(): lax.all_to_all(partials, 'par', split_axis=3, concat_axis=2, tiled=True)  43.1 us
    unnamed x11, local copies, waits for them, and re-layouts  25.1 us
    all_gather x1, waiting for transfers between devices, on_device(): all_mixing = lax.all_gather(mixing, 'arc', axis=0, tiled=True)  19.9 us
    dot_general x1, matrix products, on_device(): jnp.einsum('acij,acjk->acik', all_mixing, raw_cols.astype(jnp.float32), p...  18.1 us
    all_to_all x2, local copies, waits for them, and re-layouts, on_device(): lax.all_to_all(partials, 'par', split_axis=3, concat_axis=2, tiled=True)  13.6 us
  transfers between devices with their start and end apart: 3, of which 3 were waited for; matrix products, arithmetic and copies ran while one was open for 5% of the time, Pallas kernels for 0%

commit v1 on v0

--- a/solution.py
+++ b/solution.py
@@ -35,7 +35,10 @@
     row_block = param_count // arc_count
     row_scale = 1.0 / math.sqrt(3 * epochs * total_arcs)
     mixing = mixing_matrices(epoch_index, whitening, epochs, row_scale)
-    columns = lax.all_to_all(partials, "par", split_axis=3, concat_axis=2, tiled=True)
+    columns = jnp.concatenate(
+        lax.all_to_all(jnp.stack(jnp.split(partials, lax.axis_size("par"), axis=3)), "par", 0, 0),
+        axis=2,
+    )
     arc_position = lax.axis_index("arc")
     holder = arc_position * row_block // col_block
     offset = arc_position * row_block - holder * col_block

time: 511 us -> 474 us (0.928)
  local copies, waits for them, and re-layouts: 39.5 us -> 3.57 us
    unnamed x11 -> x8, local copies, waits for them, and re-layouts: 25.1 us -> 0.02 us
    all_to_all x2 -> x1, local copies, waits for them, and re-layouts: 13.6 us -> 1.24 us  [on_device(): lax.all_to_all(jnp.stack(jnp.split(partials, lax.axis_size('par'), axis=3...]
  transfers between devices with their start and end apart: 3 -> 3, of which waited for: 3 -> 3; matrix products, arithmetic and copies ran while one was open for 5% -> 6% of each run, Pallas kernels for 0% -> 0%
where the time goes in v1:
time: 474 us
  waiting for transfers between devices  297 us (63%)
  matrix products  109 us (23%)
  blocking collectives  43.1 us (9%)
  between operations  13.2 us (3%)
  other arithmetic  7.74 us (2%)
    psum x1, waiting for transfers between devices, from_root(): return lax.psum(block, axis)  207 us
    dot_general x1, matrix products, on_device(): lax.dot_general(row_flat, col_flat, (((0,), (0,)), ((), ())), precision=l...  82.4 us
    all_gather x1, waiting for transfers between devices, on_device(): raw_cols = lax.all_gather(columns, 'arc', axis=0, tiled=True)  69.9 us
    all_to_all x1, blocking collectives, on_device(): lax.all_to_all(jnp.stack(jnp.split(partials, lax.axis_size('par'), axis=3...  43.1 us
    all_gather x1, waiting for transfers between devices, on_device(): all_mixing = lax.all_gather(mixing, 'arc', axis=0, tiled=True)  19.9 us
    dot_general x1, matrix products, on_device(): jnp.einsum('acij,acjk->acik', all_mixing, raw_cols.astype(jnp.float32), p...  18 us
  transfers between devices with their start and end apart: 3, of which 3 were waited for; matrix products, arithmetic and copies ran while one was open for 6% of the time, Pallas kernels for 0%

profile of v1, /device:TPU:0, one launch (start us, length us, event | category | flops | bytes accessed | tf_op | source)
XLA Modules:
  0.0 474.0 jit_solution(11208053893769226909)
XLA Ops:
  6.5 0.0 copy-start
  6.5 0.0 all-gather.4.cloned.1.call-start
  6.5 1.5 slice_bitcast_fusion.3
  8.0 0.0 copy-start.3
  8.1 0.2 pad_maximum_fusion
  8.3 43.1 %all_to_all.5 = bf16[4,1,3,32,2048]{4,3,2,1,0:T(8,128)(2,1)S(1)} all-to-all(bf16[4,1,3,32,2048]{4,3,2,1,0:T(8,128)(2,1)S(1)} %pad_maximum_fusion), channel_id=1, replica_groups=mesh['arc'=8,'par'=4] {'par'}, dimensions={0} | all-to-all | bytes 3145728 | tf_op jit(solution)/shard_map/all_to_all | solution.py:39
  51.4 1.2 copy.5
  52.6 0.0 all-gather.4.cloned.1.call-update
  52.6 0.0 all-gather.6.cloned.1.call-start
  52.7 0.0 copy-done.3
  52.7 0.0 copy-done
  52.7 0.4 fusion
  53.1 0.8 copy.4
  54.0 0.0 all-gather.6.cloned.1.call-update
  54.0 0.0 all-reduce.2.cloned.1.call-start
  54.1 69.9 %all-gather.4.cloned.1.call-done = bf16[8,3,128,2048]{3,2,1,0:T(8,128)(2,1)} async-done(((bf16[1,3,128,2048]{3,2,1,0:T(8,128)(2,1)}), bf16[8,3,128,2048]{3,2,1,0:T(8,128)(2,1)}) %all-gather.4.cloned.1.call-update) | async-done | bytes 12582928 | tf_op jit(solution)/shard_map/all_gather | solution.py:45
  123.9 7.5 %dynamic-slice_select_fusion = bf16[8,3,128,1024]{3,2,1,0:T(8,128)(2,1)} fusion(bf16[8,3,128,2048]{3,2,1,0:T(8,128)(2,1)} %all-gather.4.cloned.1.call-done, s32[]{:T(128)S(6)} %select_n.18, pred[]{:T(512)S(6)} %eq.22), kind=kLoop, calls=%fused_computation | loop fusion | flops 3145728 | bytes 12582917 | tf_op jit(solution)/shard_map/jit(_where)/select_n | solution.py:11
  131.5 0.0 all-reduce.2.cloned.1.call-update
  131.5 19.9 %all-gather.6.cloned.1.call-done = f32[24,128,128]{2,1,0:T(8,128)} async-done(((f32[3,128,128]{2,1,0:T(8,128)}), f32[24,128,128]{2,1,0:T(8,128)}) %all-gather.6.cloned.1.call-update) | async-done | bytes 1572880 | tf_op jit(solution)/shard_map/all_gather | solution.py:46
  151.4 18.0 %fusion.17 = f32[8,3,128,2048]{3,2,1,0:T(8,128)} fusion(f32[8,3,128,128]{3,2,1,0:T(8,128)} %bitcast.34, bf16[8,3,128,2048]{3,2,1,0:T(8,128)(2,1)} %all-gather.4.cloned.1.call-done), kind=kOutput, calls=%fused_computation.27 | convolution fusion | flops 9663676416 | bytes 39321600 | tf_op jit(solution)/shard_map/acij,acjk->acik/dot_general | solution.py:47
  169.4 207.3 %all-reduce.2.cloned.1.call-done = bf16[8,3,128,1024]{3,2,1,0:T(8,128)(2,1)} async-done(((bf16[8,3,128,1024]{3,2,1,0:T(8,128)(2,1)}), bf16[8,3,128,1024]{3,2,1,0:T(8,128)(2,1)}) %all-reduce.2.cloned.1.call-update) | async-done | bytes 6291472 | tf_op jit(solution)/shard_map/psum | solution.py:12
  376.7 8.3 %fusion.16 = f32[8,3,128,1024]{2,3,1,0:T(8,128)S(1)} fusion(f32[8,3,128,128]{3,2,1,0:T(8,128)S(1)} %bitcast.35, bf16[8,3,128,1024]{3,2,1,0:T(8,128)(2,1)} %all-reduce.2.cloned.1.call-done), kind=kOutput, calls=%fused_computation.26 | convolution fusion | flops 4831838208 | bytes 20447232 | tf_op jit(solution)/shard_map/acij,acjk->acik/dot_general | solution.py:52
  385.0 0.0 copy-start.1
  385.1 82.4 %convolution_bitcast_fusion = f32[1024,2048]{1,0:T(8,128)} fusion(f32[8,3,128,1024]{2,3,1,0:T(8,128)S(1)} %fusion.16, f32[8,3,128,2048]{3,2,1,0:T(8,128)} %fusion.17), kind=kOutput, calls=%fused_computation.1 | convolution fusion | flops 77309411328 | bytes 46137344 | tf_op jit(solution)/shard_map/dot_general | solution.py:57
  (4 shorter events, 0.0 us)
Async XLA Ops:
  6.5 46.2 %copy-start = (f32[1,3,128,128]{3,2,1,0:T(8,128)S(1)}, f32[1,3,128,128]{3,2,1,0:T(8,128)}, u32[]{:S(2)}) copy-start(f32[1,3,128,128]{3,2,1,0:T(8,128)} %param.5) | copy-start | bytes 589828
  6.5 117.4 %all-gather.4.cloned.1.call-start = ((), (), s32[]{:S(2)}) async-start(), calls=%async_computation.1 | async-start | bytes 14155776 | tf_op jit(solution)/shard_map/all_gather | solution.py:45
  8.0 44.6 %copy-start.3 = (s32[1,128]{1,0:T(1,128)S(1)}, s32[1,128]{1,0:T(1,128)}, u32[]{:S(2)}) copy-start(s32[1,128]{1,0:T(1,128)} %param.4) | copy-start | bytes 1540
  52.6 98.8 %all-gather.6.cloned.1.call-start = ((), (), s32[]{:S(2)}) async-start(), calls=%async_computation.3 | async-start | bytes 1769472 | tf_op jit(solution)/shard_map/all_gather | solution.py:46
  54.0 322.7 %all-reduce.2.cloned.1.call-start = ((), (), s32[]{:S(2)}) async-start(), calls=%async_computation.2 | async-start | bytes 12582912 | tf_op jit(solution)/shard_map/psum | solution.py:12
  151.4 225.3 %copy-start.2 = (f32[24,128,128]{2,1,0:T(8,128)S(1)}, f32[24,128,128]{2,1,0:T(8,128)}, u32[]{:S(2)}) copy-start(f32[24,128,128]{2,1,0:T(8,128)} %all-gather.6.cloned.1.call-done) | copy-start | bytes 4718596
  385.0 82.4 %copy-start.1 = (f32[1,3,128,128]{3,2,1,0:T(8,128)S(1)}, f32[1,3,128,128]{3,2,1,0:T(8,128)}, u32[]{:S(2)}) copy-start(f32[1,3,128,128]{3,2,1,0:T(8,128)} %param.5) | copy-start | bytes 589828
Sparse Core Ops, SparseCore 0:
  52.8 71.1 all-gather.3
  125.8 25.5 all-gather.5
  153.8 222.8 all-reduce.1
